TPU v7x, 512 devices: a whole 4x4x16 slice. The times are simulated.
512 devices in a mesh: frames: 8 (over x_hi, y), queries: 64 (over x_lo, z, core).
Axes of the slice: x: 4 (x_hi: 2, x_lo: 2; x = x_hi * 2 + x_lo), y: 4, z: 16, core: 2. Of those that a mesh axis runs over, the one named last changes fastest.
Arguments:
- frame_maps: bfloat16 [16, 4096, 256], P('frames', 'queries'), may hold values from -6 to 6
- query_table: bfloat16 [8, 4096, 256], P('frames', 'queries'), may hold values from -6 to 6
- start_frame: int32 [4096], P('queries'), may hold values from 0 to 15
- row_ids: int32 [4096], P('queries'), may hold values from 0 to 63
- conv1_w: bfloat16 [3, 3, 1, 16], replicated, may hold values from -2 to 2
- conv1_b: float32 [16], replicated, may hold values from -3 to 3
- conv2_w: bfloat16 [3, 3, 16, 32], replicated, may hold values from -0.5 to 0.5
- conv2_b: float32 [32], replicated, may hold values from -3 to 3
- proj_w: bfloat16 [32, 512], replicated, may hold values from -1 to 1
- proj_b: float32 [512], replicated, may hold values from -3 to 3
- time_w: float32 [3, 512], replicated, may hold values from -3 to 3
- time_b: float32 [512], replicated, may hold values from -3 to 3
Outputs:
- track_feats: bfloat16 [4096, 16, 512], P('queries', 'frames')
Inputs may be any that keep to these rules, and one draw needn't show every extreme that they name: `start_frame`: the frame in which the query was picked, one of the 16 frames. `row_ids`: a row index within the query's own block of 64 rows.
All inputs are finite; a program needn't handle non-finite values.
Results may differ from a plain program's by a relative error of at most 0.001.
The roundings to bfloat16 on the way count: a program that leaves them out, or rounds other values in their place, can miss the bound.
Values may be sent and summed in bfloat16 or wider, within the bound.
No kernel may reach another device: no remote copies, remote signals or barrier semaphores. Data moves between devices by JAX's collectives and lax.ppermute only.
A program may use at most 64 MiB of HBM per device.

v0:
```python
import functools

import jax
import jax.numpy as jnp
from jax import lax
from jax.experimental import pallas as pl
from jax.experimental.pallas import tpu as pltpu
from jax.sharding import Mesh, PartitionSpec as P


MAP = 64
CH1 = 16
CH2 = 32
HALF1 = MAP // 2
HALF2 = MAP // 4
ROW1 = HALF1 * CH1
ROW2 = HALF2 * CH2
BF = jnp.bfloat16
F32 = jnp.float32
INTERPRET = False


def iota(shape, dim):
    return lax.broadcasted_iota(jnp.int32, shape, dim)


def in_hbm(array):
    if INTERPRET:
        return array
    return pltpu.with_memory_space_constraint(array, pltpu.HBM)


def opening_kernel(
    where_ref, maps_hbm, table_hbm, start_hbm, rows_hbm, out_ref, table, start, rows, sems
):
    frames_here, cells = maps_hbm.shape[0], maps_hbm.shape[1]
    copies = [
        pltpu.make_async_copy(start_hbm, start, sems.at[0]),
        pltpu.make_async_copy(rows_hbm, rows, sems.at[1]),
        pltpu.make_async_copy(table_hbm, table, sems.at[2]),
    ]
    for f in range(frames_here):
        part = out_ref.at[pl.ds(cells * f, cells)]
        copies.append(pltpu.make_async_copy(maps_hbm.at[f], part, sems.at[3 + f]))
    for copy in copies:
        copy.start()
    for copy in copies[:3]:
        copy.wait()
    low = where_ref[2] * frames_here
    owned = (start[...] >= low) & (start[...] < low + frames_here)
    row = jnp.where(owned, rows[...], -1)
    chosen = (iota((table.shape[1], row.shape[1]), 0) == row).astype(BF)
    got = lax.dot_general(chosen, table[0], (((0,), (0,)), ((), ())), preferred_element_type=F32)
    out_ref[frames_here * cells :, :] = got.astype(BF)
    for copy in copies[3:]:
        copy.wait()


def opening(where, frame_maps, query_table, start_frame, row_ids):
    frames_here, cells, channels = frame_maps.shape
    count = start_frame.shape[0]
    hbm = pl.BlockSpec(memory_space=pltpu.HBM)
    arrays = (frame_maps, query_table, start_frame[None, :], row_ids[None, :])
    return pl.pallas_call(
        opening_kernel,
        out_shape=jax.ShapeDtypeStruct((frames_here * cells + count, channels), BF),
        in_specs=[pl.BlockSpec(memory_space=pltpu.SMEM)] + [hbm] * 4,
        out_specs=pl.BlockSpec(memory_space=pltpu.VMEM),
        scratch_shapes=[
            pltpu.VMEM(query_table.shape, BF),
            pltpu.VMEM((1, count), jnp.int32),
            pltpu.VMEM((1, count), jnp.int32),
            pltpu.SemaphoreType.DMA((5,)),
        ],
        cost_estimate=pl.CostEstimate(flops=2_000_000, bytes_accessed=200_000, transcendentals=0),
        compiler_params=pltpu.CompilerParams(vmem_limit_bytes=4 << 20),
        interpret=INTERPRET,
    )(where, *map(in_hbm, arrays))


def pick_kernel(where_ref, all_ref, block_ref, queries_ref):
    x, core = where_ref[0], where_ref[3]
    cells = block_ref.shape[1] // 2
    frame = pl.ds(pl.multiple_of(cells * x, cells), cells)
    for c in range(2):
        for side in range(2):
            block_ref[c, cells * side : cells * (side + 1), :] = all_ref[2 * side + c, frame, :]
    count = queries_ref.shape[0] // 2
    first = 2 * cells
    queries_ref[0:count, :] = all_ref[2 * x + core, first : first + count, :]
    queries_ref[count:, :] = all_ref[2 * (1 - x) + core, first : first + count, :]


def picked(where, gathered, cells):
    channels = gathered.shape[2]
    count = gathered.shape[1] - 2 * cells
    vmem = pl.BlockSpec(memory_space=pltpu.VMEM)
    return pl.pallas_call(
        pick_kernel,
        out_shape=(
            jax.ShapeDtypeStruct((2, 2 * cells, channels), BF),
            jax.ShapeDtypeStruct((2 * count, channels), BF),
        ),
        in_specs=[pl.BlockSpec(memory_space=pltpu.SMEM), vmem],
        out_specs=(vmem, vmem),
        cost_estimate=pl.CostEstimate(flops=0, bytes_accessed=300_000, transcendentals=0),
        compiler_params=pltpu.CompilerParams(vmem_limit_bytes=4 << 20),
        interpret=INTERPRET,
    )(where, gathered)


def weights_kernel(*refs):
    a_ref, b_ref, wide1_ref, wide2_ref, w1_ref, w2_ref, bias1_ref, bias2_ref, sems = refs[4:]
    copies = [
        pltpu.make_async_copy(refs[k], refs[8 + k], sems.at[k]) for k in range(4)
    ]
    for copy in copies:
        copy.start()
    b_ref[...] = jnp.zeros(b_ref.shape, BF)
    for copy in copies:
        copy.wait()
    spread = (iota((CH1, ROW1), 1) % CH1 == iota((CH1, ROW1), 0)).astype(BF)
    wide1_ref[...] = jnp.concatenate([bias1_ref[...]] * HALF1, axis=1)
    wide2_ref[...] = jnp.concatenate([bias2_ref[...]] * HALF2, axis=1)

    in_x = iota((MAP, ROW1), 0)
    out_x = iota((MAP, ROW1), 1) // CH1
    a_ref[0:MAP, :] = jnp.zeros((MAP, ROW1), BF)
    for dy in range(3):
        wide = jnp.dot(w1_ref[dy], spread, preferred_element_type=F32)
        block = jnp.zeros((MAP, ROW1), F32)
        for dx in range(3):
            block = jnp.where(in_x == 2 * out_x + dx - 1, wide[dx : dx + 1, :], block)
        a_ref[MAP * (dy + 1) : MAP * (dy + 2), :] = block.astype(BF)

    for dy in range(3):
        taps = jnp.concatenate([w2_ref[3 * dy + dx] for dx in range(3)], axis=0)
        taps = jnp.concatenate([taps] * (128 // CH2), axis=1)
        for out_x in range(HALF2):
            low = 2 * out_x - 1
            skip = max(0, -low)
            lane = CH2 * out_x
            part = lane % 128
            b_ref[
                ROW1 * dy + CH1 * (low + skip) : ROW1 * dy + CH1 * (low + 3), lane : lane + CH2
            ] = taps[CH1 * skip :, part : part + CH2]


def banded_weights(conv1_w, conv1_b, conv2_w, conv2_b):
    return pl.pallas_call(
        weights_kernel,
        out_shape=(
            jax.ShapeDtypeStruct((4 * MAP, ROW1), BF),
            jax.ShapeDtypeStruct((3 * ROW1, ROW2), BF),
            jax.ShapeDtypeStruct((1, ROW1), F32),
            jax.ShapeDtypeStruct((1, ROW2), F32),
        ),
        in_specs=[pl.BlockSpec(memory_space=pltpu.HBM)] * 4,
        scratch_shapes=[
            pltpu.VMEM((3, 3, CH1), BF),
            pltpu.VMEM((9, CH1, CH2), BF),
            pltpu.VMEM((1, CH1), F32),
            pltpu.VMEM((1, CH2), F32),
            pltpu.SemaphoreType.DMA((4,)),
        ],
        cost_estimate=pl.CostEstimate(flops=50_000_000, bytes_accessed=2_000_000, transcendentals=0),
        compiler_params=pltpu.CompilerParams(vmem_limit_bytes=8 << 20),
        interpret=INTERPRET,
    )(
        *map(
            in_hbm,
            (
                jnp.transpose(conv1_w, (0, 2, 1, 3)).reshape(3, 3, CH1),
                conv2_w.reshape(9, CH1, CH2),
                conv1_b[None, :],
                conv2_b[None, :],
            ),
        )
    )


def join_kernel(*refs):
    low = 0
    for ref in refs[:-1]:
        high = low + ref.shape[0]
        refs[-1][low:high] = ref[...]
        low = high


def joined(*blocks):
    count = sum(block.shape[0] for block in blocks)
    vmem = pl.BlockSpec(memory_space=pltpu.VMEM)
    shape = (count,) + blocks[0].shape[1:]
    return pl.pallas_call(
        join_kernel,
        out_shape=jax.ShapeDtypeStruct(shape, BF),
        in_specs=[vmem] * len(blocks),
        out_specs=vmem,
        cost_estimate=pl.CostEstimate(flops=0, bytes_accessed=300_000, transcendentals=0),
        compiler_params=pltpu.CompilerParams(vmem_limit_bytes=4 << 20),
        interpret=INTERPRET,
    )(*blocks)


def trim_kernel(where_ref, blocks_ref, out_ref):
    out_ref[0:2] = blocks_ref[0:2]
    out_ref[2] = blocks_ref[2 + where_ref[3]]


def trimmed(where, blocks):
    vmem = pl.BlockSpec(memory_space=pltpu.VMEM)
    return pl.pallas_call(
        trim_kernel,
        out_shape=jax.ShapeDtypeStruct((3,) + blocks.shape[1:], BF),
        in_specs=[pl.BlockSpec(memory_space=pltpu.SMEM), vmem],
        out_specs=vmem,
        cost_estimate=pl.CostEstimate(flops=0, bytes_accessed=300_000, transcendentals=0),
        compiler_params=pltpu.CompilerParams(vmem_limit_bytes=4 << 20),
        interpret=INTERPRET,
    )(where, blocks)


def correlate(corr, q, z, z_count, low, high, shift):
    chip = lax.rem(z + z_count + shift, z_count)
    cells = jnp.concatenate([low[0:MAP], high[0:MAP], low[MAP:], high[MAP:]], axis=0)
    got = lax.dot_general(q, cells, (((1,), (1,)), ((), ())), preferred_element_type=F32)
    got = (got * 0.0625).astype(BF)
    for side in range(2):
        part = got[:, 128 * side : 128 * (side + 1)]
        y = side * z_count + chip
        corr[y, :, 128:256] = part
        corr[y + 1, :, 0:128] = part


def corr_kernel(z_count, where_ref, q_ref, own_ref, *refs):
    *mine_refs, corr = refs
    z = where_ref[1]
    toward = 2 * where_ref[3] - 1
    q = q_ref[...]
    corr[...] = jnp.zeros(corr.shape, BF)
    correlate(corr, q, z, z_count, own_ref[0], own_ref[1], 0)
    distance = 0
    for ref in mine_refs:
        for k in range(0, ref.shape[0], 2):
            distance += 1
            correlate(corr, q, z, z_count, ref[k], ref[k + 1], toward * distance)


def partial_corr(where, queries, own, blocks):
    vmem = pl.BlockSpec(memory_space=pltpu.VMEM)
    return pl.pallas_call(
        functools.partial(corr_kernel, MAP // 4),
        out_shape=jax.ShapeDtypeStruct((HALF1 + 1, queries.shape[0], 256), BF),
        in_specs=[pl.BlockSpec(memory_space=pltpu.SMEM)] + [vmem] * (2 + len(blocks)),
        out_specs=vmem,
        cost_estimate=pl.CostEstimate(
            flops=250_000_000, bytes_accessed=4_000_000, transcendentals=0
        ),
        compiler_params=pltpu.CompilerParams(vmem_limit_bytes=12 << 20),
        interpret=INTERPRET,
    )(where, queries, own, *blocks)


def cost_kernel(z_count, where_ref, q_ref, last_ref, old_ref, cross_ref, *refs):
    del old_ref
    a_ref, b_ref, bias1_ref, bias2_ref, kept_ref, sent_ref, corr, hid, acc = refs
    z = where_ref[1]
    n = q_ref.shape[0]
    hid[0, :, 0:ROW1] = jnp.zeros((n, ROW1), BF)
    q = q_ref[...]
    away = 1 - 2 * where_ref[3]
    for k in range(0, cross_ref.shape[0], 2):
        correlate(corr, q, z, z_count, cross_ref[k], cross_ref[k + 1], away * (k // 2 + 1))
    correlate(corr, q, z, z_count, last_ref[0], last_ref[1], -7)
    correlate(corr, q, z, z_count, last_ref[3], last_ref[4], 7)
    correlate(corr, q, z, z_count, last_ref[2], last_ref[5], 8)

    bias1 = bias1_ref[...]
    rows1 = 8
    for t in range(HALF1 // rows1):
        lhs = corr[rows1 * t : rows1 * (t + 1)].reshape(rows1 * n, 256)
        got = jnp.dot(lhs, a_ref[...], preferred_element_type=F32)
        got = jnp.maximum(got + bias1, 0.0).astype(BF).reshape(rows1, n, ROW1)
        for s in range(rows1):
            y = rows1 * t + s
            j = y // 2
            if y % 2 == 0:
                hid[j, :, ROW1 : 2 * ROW1] = got[s]
            else:
                hid[j, :, 2 * ROW1 : 3 * ROW1] = got[s]
                hid[j + 1, :, 0:ROW1] = got[s]

    bias2 = bias2_ref[...]
    half = ROW2 // 2
    rows2 = 4
    acc[...] = jnp.zeros(acc.shape, F32)
    for t in range(HALF2 // rows2):
        tile = slice(rows2 * t, rows2 * (t + 1))
        left = jnp.zeros((rows2 * n, half), F32)
        for dy in range(3):
            k = slice(ROW1 * dy, ROW1 * dy + ROW1 // 2)
            left += jnp.dot(
                hid[tile, :, k].reshape(rows2 * n, ROW1 // 2),
                b_ref[k, 0:half],
                preferred_element_type=F32,
            )
        right = jnp.dot(
            hid[tile].reshape(rows2 * n, 3 * ROW1), b_ref[:, half:], preferred_element_type=F32
        )
        left = jnp.maximum(left + bias2[:, :half], 0.0).reshape(rows2, n, half)
        right = jnp.maximum(right + bias2[:, half:], 0.0).reshape(rows2, n, half)
        acc[:, :half] += jnp.sum(left, axis=0)
        acc[:, half:] += jnp.sum(right, axis=0)
    total = acc[:, 0:128]
    for k in range(1, ROW2 // 128):
        total = total + acc[:, 128 * k : 128 * (k + 1)]
    total = (total[:, 0:32] + total[:, 32:64]) + (total[:, 64:96] + total[:, 96:128])
    pooled = (total * (1.0 / (HALF2 * HALF2))).astype(BF)
    kept_ref[...] = pooled[: n // 2]
    sent_ref[...] = pooled[n // 2 :]


def pooled_costs(where, queries, last, corr, cross, a, b, bias1, bias2):
    n = queries.shape[0]
    vmem = pl.BlockSpec(memory_space=pltpu.VMEM)
    return pl.pallas_call(
        functools.partial(cost_kernel, MAP // 4),
        out_shape=(jax.ShapeDtypeStruct((n // 2, CH2), BF),) * 2
        + (jax.ShapeDtypeStruct(corr.shape, BF),),
        in_specs=[pl.BlockSpec(memory_space=pltpu.SMEM)] + [vmem] * 8,
        out_specs=(vmem,) * 3,
        scratch_shapes=[
            pltpu.VMEM((HALF2 + 1, n, 3 * ROW1), BF),
            pltpu.VMEM((n, ROW2), F32),
        ],
        input_output_aliases={3: 2},
        cost_estimate=pl.CostEstimate(
            flops=5_000_000_000, bytes_accessed=4_000_000, transcendentals=0
        ),
        compiler_params=pltpu.CompilerParams(vmem_limit_bytes=28 << 20),
        interpret=INTERPRET,
    )(where, queries, last, corr, cross, a, b, bias1, bias2)[:2]


def tail_kernel(
    frame_count,
    where_ref,
    kept_ref,
    partner_ref,
    straight_ref,
    crossed_ref,
    proj_w_ref,
    proj_b_ref,
    time_w_ref,
    time_b_ref,
    out_ref,
):
    x, frame_block = where_ref[0], where_ref[2]
    first = x == 0
    kept, partner = kept_ref[...], partner_ref[...]
    straight, crossed = straight_ref[...], crossed_ref[...]
    around = [
        jnp.where(first, crossed, straight),
        jnp.where(first, kept, partner),
        jnp.where(first, partner, kept),
        jnp.where(first, straight, crossed),
    ]
    valid = [frame_block > 0, None, None, frame_block < frame_count - 1]
    wide = []
    for pooled, there in zip(around, valid):
        got = jnp.dot(pooled, proj_w_ref[...], preferred_element_type=F32) + proj_b_ref[...]
        got = got.astype(BF).astype(F32)
        if there is not None:
            got = jnp.where(there, got, 0.0)
        wide.append(got)
    for t in range(2):
        mixed = (
            time_w_ref[0:1, :] * wide[t]
            + time_w_ref[1:2, :] * wide[t + 1]
            + time_w_ref[2:3, :] * wide[t + 2]
            + time_b_ref[...]
        )
        out_ref[:, t, :] = mixed.astype(BF)


def tail(frame_count, where, pooled, proj_w, proj_b, time_w, time_b):
    count, width = pooled[0].shape[0], proj_w.shape[1]
    vmem = pl.BlockSpec(memory_space=pltpu.VMEM)
    return pl.pallas_call(
        functools.partial(tail_kernel, frame_count),
        out_shape=jax.ShapeDtypeStruct((count, 2, width), BF),
        in_specs=[pl.BlockSpec(memory_space=pltpu.SMEM)] + [vmem] * 8,
        out_specs=vmem,
        compiler_params=pltpu.CompilerParams(vmem_limit_bytes=8 << 20),
        interpret=INTERPRET,
    )(where, *pooled, proj_w, proj_b[None, :], time_w, time_b[None, :])


def one_device(
    sizes,
    frame_maps,
    query_table,
    start_frame,
    row_ids,
    conv1_w,
    conv1_b,
    conv2_w,
    conv2_b,
    proj_w,
    proj_b,
    time_w,
    time_b,
):
    xh_count, y_count, _, z_count, _ = sizes
    frame_count = xh_count * y_count
    x = lax.axis_index("xl")
    z = lax.axis_index("z")
    frame_block = lax.axis_index("xh") * y_count + lax.axis_index("y")
    where = jnp.stack([x, z, frame_block, lax.axis_index("c")]).astype(jnp.int32)
    swap = [(0, 1), (1, 0)]

    def flip(axis, count, step):
        return lambda v: lax.ppermute(v, axis, [(i, i ^ step) for i in range(count)])

    def along(block, distance):
        pairs = []
        for i in range(z_count):
            pairs.append((2 * i, 2 * ((i + distance) % z_count)))
            pairs.append((2 * i + 1, 2 * ((i - distance) % z_count) + 1))
        return lax.ppermute(block, ("z", "c"), pairs)

    def both(block):
        return lax.all_gather(block, "c", axis=0, tiled=True)

    def behind(value, earlier):
        return lax.optimization_barrier((value, earlier))[0]

    message = opening(where, frame_maps, query_table, start_frame, row_ids)
    gathered = lax.all_gather(message, ("xl", "c"), axis=0)
    own, queries = picked(where, gathered, frame_maps.shape[1])
    weights = banded_weights(conv1_w, conv1_b, conv2_w, conv2_b)
    near = []
    for distance in (1, 2):
        near.append(along(own, distance))
    queries = queries + flip("y", y_count, 1)(queries)
    near = lax.optimization_barrier(near)

    ring = [joined(*near)]
    ring.append(along(ring[0], 2))
    if y_count > 2:
        queries = queries + flip("y", y_count, 2)(behind(queries, ring[0]))
    ring[1], weights = lax.optimization_barrier((ring[1], weights))

    ring.append(along(ring[1], 2))
    if xh_count > 1:
        queries = queries + flip("xh", xh_count, 1)(behind(queries, ring[1]))
    ring[2] = lax.optimization_barrier(ring[2])

    end = trimmed(where, ring[2])
    last = along(end, 2)
    cross = lax.ppermute(joined(*ring), "c", swap)
    corr = partial_corr(where, queries, own, ring)
    last, corr = lax.optimization_barrier((last, corr))

    kept, sent = pooled_costs(where, queries, both(last), corr, cross, *weights)

    def frame_pairs(cross):
        pairs = []
        for f in range(frame_count):
            if f > 0:
                pairs.append((2 * (f - 1) + 1, 2 * f + (0 if cross else 1)))
            if f < frame_count - 1:
                pairs.append((2 * (f + 1), 2 * f + (1 if cross else 0)))
        return pairs

    partner = lax.ppermute(sent, "xl", swap)
    straight = lax.ppermute(kept, ("xh", "y", "xl"), frame_pairs(False))
    crossed = lax.ppermute(sent, ("xh", "y", "xl"), frame_pairs(True))
    pooled = (kept, partner, straight, crossed)
    return tail(frame_count, where, pooled, proj_w, proj_b, time_w, time_b)


def solution(mesh):

    frames, _ = mesh.devices.shape
    sizes = (frames // 4 or 1, min(frames, 4), 2, MAP // 4, 2)
    fine = Mesh(mesh.devices.reshape(sizes), ("xh", "y", "xl", "z", "c"))
    fr = ("xh", "y")
    qs = ("xl", "z", "c")
    placed = (P(fr, qs, None), P(fr, qs, None), P(qs), P(qs)) + (P(),) * 8
    return jax.shard_map(
        functools.partial(one_device, sizes),
        mesh=fine,
        in_specs=placed,
        out_specs=P(qs, fr, None),
        check_vma=False,
    )
```

profile of v0, /device:TPU:68, one launch (start us, length us, event | category | flops | bytes accessed | tf_op | source)
XLA Modules:
  0.0 99.5 jit_solution(1951639801824719263)
XLA Ops:
  0.1 1.6 %shard_map.118 = bf16[192,256]{1,0:T(8,128)(2,1)S(1)} custom-call(s32[4]{0:T(128)S(1)} %pad_add_fusion.where_ref, bf16[2,64,256]{2,1,0:T(8,128)(2,1)} %maps_hbm.1, bf16[1,64,256]{2,1,0:T(8,128)(2,1)} %table_hbm.1, s32[1,64]{1,0:T(1,128)} %bitcast.16, s32[1,64]{1,0:T(1,128)} %bitcast.17), custom_call_target="tpu_custom_call" | custom-call | flops 2000000 | bytes 200000 | tf_op jit(solution)/shard_map/pallas_call | solution.py:64
  1.7 6.2 %all-gather = bf16[768,256]{1,0:T(8,128)(2,1)S(1)} all-gather(bf16[192,256]{1,0:T(8,128)(2,1)S(1)} %shard_map.118), channel_id=2, replica_groups=mesh['xh'=2,'y'=4,'xl'=2,'z'=16,'c'=2] {'xl','c'}, dimensions={0}, use_global_device_ids=true | all-gather | bytes 491520 | tf_op jit(solution)/shard_map/all_gather | solution.py:439
  8.4 6.4 %collective-permute-start.2 = (bf16[2,128,256]{2,1,0:T(8,128)(2,1)S(1)}, bf16[2,128,256]{2,1,0:T(8,128)(2,1)S(1)}, u32[]{:S(2)}, u32[]{:S(2)}) collective-permute-start(bf16[2,128,256]{2,1,0:T(8,128)(2,1)S(1)} %get-tuple-element.25.own_ref), channel_id=1, source_target_pairs={{0,4},{1,29},{2,6},{3,31},{4,8},{5,1},{6,10},{7,3},{8,12},{9,5},{1... | collective-permute-start | bytes 393224 | tf_op jit(solution)/shard_map/ppermute | solution.py:430
  14.8 3.8 %collective-permute-start.1 = (bf16[2,128,256]{2,1,0:T(8,128)(2,1)S(1)}, bf16[2,128,256]{2,1,0:T(8,128)(2,1)S(1)}, u32[]{:S(2)}, u32[]{:S(2)}) collective-permute-start(bf16[2,128,256]{2,1,0:T(8,128)(2,1)S(1)} %get-tuple-element.25.own_ref), channel_id=1, source_target_pairs={{0,2},{1,31},{2,4},{3,1},{4,6},{5,3},{6,8},{7,5},{8,10},{9,7},{10,... | collective-permute-start | bytes 393224 | tf_op jit(solution)/shard_map/ppermute | solution.py:430
  18.6 3.0 %collective-permute-done.1.refs_0_ = bf16[2,128,256]{2,1,0:T(8,128)(2,1)S(1)} collective-permute-done((bf16[2,128,256]{2,1,0:T(8,128)(2,1)S(1)}, bf16[2,128,256]{2,1,0:T(8,128)(2,1)S(1)}, u32[]{:S(2)}, u32[]{:S(2)}) %collective-permute-start.1) | collective-permute-done | bytes 131104 | tf_op jit(solution)/shard_map/ppermute | solution.py:430
  21.7 6.4 %collective-permute-start.4 = (bf16[4,128,256]{2,1,0:T(8,128)(2,1)S(1)}, bf16[4,128,256]{2,1,0:T(8,128)(2,1)S(1)}, u32[]{:S(2)}, u32[]{:S(2)}) collective-permute-start(bf16[4,128,256]{2,1,0:T(8,128)(2,1)S(1)} %shard_map.120.refs_0_), channel_id=1, source_target_pairs={{0,4},{1,29},{2,6},{3,31},{4,8},{5,1},{6,10},{7,3},{8,12},{9,5},{1... | collective-permute-start | bytes 786440 | tf_op jit(solution)/shard_map/ppermute | solution.py:430
  29.2 5.3 %collective-permute-done.4.refs_1_ = bf16[4,128,256]{2,1,0:T(8,128)(2,1)S(1)} collective-permute-done((bf16[4,128,256]{2,1,0:T(8,128)(2,1)S(1)}, bf16[4,128,256]{2,1,0:T(8,128)(2,1)S(1)}, u32[]{:S(2)}, u32[]{:S(2)}) %collective-permute-start.4) | collective-permute-done | bytes 262176 | tf_op jit(solution)/shard_map/ppermute | solution.py:430
  34.5 6.5 %collective-permute-start.6 = (bf16[4,128,256]{2,1,0:T(8,128)(2,1)S(1)}, bf16[4,128,256]{2,1,0:T(8,128)(2,1)S(1)}, u32[]{:S(2)}, u32[]{:S(2)}) collective-permute-start(bf16[4,128,256]{2,1,0:T(8,128)(2,1)S(1)} %collective-permute-done.4.refs_1_), channel_id=1, source_target_pairs={{0,4},{1,29},{2,6},{3,31},{4,8},{5,1},{6,10},{7,3},{8,12},{9,5},{1... | collective-permute-start | bytes 786440 | tf_op jit(solution)/shard_map/ppermute | solution.py:430
  41.0 6.6 %collective-permute-done.6.blocks_ref.refs_2_ = bf16[4,128,256]{2,1,0:T(8,128)(2,1)S(1)} collective-permute-done((bf16[4,128,256]{2,1,0:T(8,128)(2,1)S(1)}, bf16[4,128,256]{2,1,0:T(8,128)(2,1)S(1)}, u32[]{:S(2)}, u32[]{:S(2)}) %collective-permute-start.6) | collective-permute-done | bytes 262176 | tf_op jit(solution)/shard_map/ppermute | solution.py:430
  47.6 1.9 %collective-permute-start.8 = (bf16[12,128,256]{2,1,0:T(8,128)(2,1)S(1)}, bf16[12,128,256]{2,1,0:T(8,128)(2,1)S(1)}, u32[]{:S(2)}, u32[]{:S(2)}) collective-permute-start(bf16[12,128,256]{2,1,0:T(8,128)(2,1)S(1)} %shard_map.124), channel_id=1, source_target_pairs={{0,1},{1,0},{2,3},{3,2},{4,5},{5,4},{6,7},{7,6},{8,9},{9,8},{10,11... | collective-permute-start | bytes 2359304 | tf_op jit(solution)/shard_map/ppermute | solution.py:461
  49.6 3.5 %collective-permute-start = (bf16[128,256]{1,0:T(8,128)(2,1)S(1)}, bf16[128,256]{1,0:T(8,128)(2,1)S(1)}, u32[]{:S(2)}, u32[]{:S(2)}) collective-permute-start(bf16[128,256]{1,0:T(8,128)(2,1)S(1)} %get-tuple-element.24), channel_id=1, source_target_pairs={{0,64},{64,0},{128,192},{192,128},{1,65},{65,1},{129,193},{193,129... | collective-permute-start | bytes 196616 | tf_op jit(solution)/shard_map/ppermute | solution.py:423
  53.6 6.6 %collective-permute-start.7 = (bf16[3,128,256]{2,1,0:T(8,128)(2,1)S(1)}, bf16[3,128,256]{2,1,0:T(8,128)(2,1)S(1)}, u32[]{:S(2)}, u32[]{:S(2)}) collective-permute-start(bf16[3,128,256]{2,1,0:T(8,128)(2,1)S(1)} %shard_map.122), channel_id=1, source_target_pairs={{0,4},{1,29},{2,6},{3,31},{4,8},{5,1},{6,10},{7,3},{8,12},{9,5},{1... | collective-permute-start | bytes 589832 | tf_op jit(solution)/shard_map/ppermute | solution.py:430
  60.2 4.8 %collective-permute-start.3 = (bf16[128,256]{1,0:T(8,128)(2,1)S(1)}, bf16[128,256]{1,0:T(8,128)(2,1)S(1)}, u32[]{:S(2)}, u32[]{:S(2)}) collective-permute-start(bf16[128,256]{1,0:T(8,128)(2,1)S(1)} %add.13), channel_id=1, source_target_pairs={{0,128},{64,192},{128,0},{192,64},{1,129},{65,193},{129,1},{193,65... | collective-permute-start | bytes 196616 | tf_op jit(solution)/shard_map/ppermute | solution.py:423
  65.0 2.8 %collective-permute-done.3 = bf16[128,256]{1,0:T(8,128)(2,1)S(1)} collective-permute-done((bf16[128,256]{1,0:T(8,128)(2,1)S(1)}, bf16[128,256]{1,0:T(8,128)(2,1)S(1)}, u32[]{:S(2)}, u32[]{:S(2)}) %collective-permute-start.3) | collective-permute-done | bytes 65568 | tf_op jit(solution)/shard_map/ppermute | solution.py:423
  67.9 2.7 %collective-permute-start.5 = (bf16[128,256]{1,0:T(8,128)(2,1)S(1)}, bf16[128,256]{1,0:T(8,128)(2,1)S(1)}, u32[]{:S(2)}, u32[]{:S(2)}) collective-permute-start(bf16[128,256]{1,0:T(8,128)(2,1)S(1)} %add.14), channel_id=1, source_target_pairs={{0,256},{256,0},{1,257},{257,1},{2,258},{258,2},{3,259},{259,3},{4... | collective-permute-start | bytes 196616 | tf_op jit(solution)/shard_map/ppermute | solution.py:423
  70.6 4.9 %collective-permute-done.5 = bf16[128,256]{1,0:T(8,128)(2,1)S(1)} collective-permute-done((bf16[128,256]{1,0:T(8,128)(2,1)S(1)}, bf16[128,256]{1,0:T(8,128)(2,1)S(1)}, u32[]{:S(2)}, u32[]{:S(2)}) %collective-permute-start.5) | collective-permute-done | bytes 65568 | tf_op jit(solution)/shard_map/ppermute | solution.py:423
  76.6 2.1 %all_gather.11.last_ref = bf16[6,128,256]{2,1,0:T(8,128)(2,1)S(1)} all-gather(bf16[3,128,256]{2,1,0:T(8,128)(2,1)S(1)} %collective-permute-done.7), channel_id=1, replica_groups=mesh['xh'=2,'y'=4,'xl'=2,'z'=16,'c'=2] {'c'}, dimensions={0}, use_global_device_ids=true | all-gather | bytes 589824 | tf_op jit(solution)/shard_map/all_gather | solution.py:433
  78.8 5.0 %shard_map.125 = (bf16[64,32]{1,0:T(8,128)(2,1)S(1)}, bf16[64,32]{1,0:T(8,128)(2,1)S(1)}, bf16[33,128,256]{2,1,0:T(8,128)(2,1)S(1)}) custom-call(s32[4]{0:T(128)S(1)} %pad_add_fusion.where_ref, bf16[128,256]{1,0:T(8,128)(2,1)S(1)} %add.15.q_ref, bf16[6,128,256]{2,1,0:T(8,128)(2,1)S(1)} %all_gather.11.last_ref, ...), custom_call_target="tpu_custom_call", output_to_operand_aliasing={{2}: (3, {})} | custom-call | flops 5000000000 | bytes 4000000 | tf_op jit(solution)/shard_map/pallas_call | solution.py:326
  83.8 4.3 %collective-permute-start.10 = (bf16[64,32]{1,0:T(8,128)(2,1)S(1)}, bf16[64,32]{1,0:T(8,128)(2,1)S(1)}, u32[]{:S(2)}, u32[]{:S(2)}) collective-permute-start(bf16[64,32]{1,0:T(8,128)(2,1)S(1)} %get-tuple-element.41.kept_ref), channel_id=1, source_target_pairs={{64,0},{32,96},{128,64},{96,160},{192,128},{160,224},{256,192},{22... | collective-permute-start | bytes 12296 | tf_op jit(solution)/shard_map/ppermute | solution.py:477
  88.1 4.2 %collective-permute-start.11 = (bf16[64,32]{1,0:T(8,128)(2,1)S(1)}, bf16[64,32]{1,0:T(8,128)(2,1)S(1)}, u32[]{:S(2)}, u32[]{:S(2)}) collective-permute-start(bf16[64,32]{1,0:T(8,128)(2,1)S(1)} %get-tuple-element.42), channel_id=1, source_target_pairs={{64,32},{32,64},{128,96},{96,128},{192,160},{160,192},{256,224},{2... | collective-permute-start | bytes 12296 | tf_op jit(solution)/shard_map/ppermute | solution.py:478
  92.4 1.9 %collective-permute-start.9 = (bf16[64,32]{1,0:T(8,128)(2,1)S(1)}, bf16[64,32]{1,0:T(8,128)(2,1)S(1)}, u32[]{:S(2)}, u32[]{:S(2)}) collective-permute-start(bf16[64,32]{1,0:T(8,128)(2,1)S(1)} %get-tuple-element.42), channel_id=1, source_target_pairs={{0,32},{32,0},{1,33},{33,1},{2,34},{34,2},{3,35},{35,3},{4,36},{36... | collective-permute-start | bytes 12296 | tf_op jit(solution)/shard_map/ppermute | solution.py:476
  94.3 1.6 %collective-permute-done.11.crossed_ref = bf16[64,32]{1,0:T(8,128)(2,1)S(1)} collective-permute-done((bf16[64,32]{1,0:T(8,128)(2,1)S(1)}, bf16[64,32]{1,0:T(8,128)(2,1)S(1)}, u32[]{:S(2)}, u32[]{:S(2)}) %collective-permute-start.11) | collective-permute-done | bytes 4128 | tf_op jit(solution)/shard_map/ppermute | solution.py:478
  95.9 2.1 %collective-permute-done.9.partner_ref = bf16[64,32]{1,0:T(8,128)(2,1)S(1)} collective-permute-done((bf16[64,32]{1,0:T(8,128)(2,1)S(1)}, bf16[64,32]{1,0:T(8,128)(2,1)S(1)}, u32[]{:S(2)}, u32[]{:S(2)}) %collective-permute-start.9) | collective-permute-done | bytes 4128 | tf_op jit(solution)/shard_map/ppermute | solution.py:476
  98.0 1.5 %shard_map.126 = bf16[64,2,512]{2,1,0:T(2,128)(2,1)} custom-call(s32[4]{0:T(128)S(1)} %pad_add_fusion.where_ref, bf16[64,32]{1,0:T(8,128)(2,1)S(1)} %get-tuple-element.41.kept_ref, bf16[64,32]{1,0:T(8,128)(2,1)S(1)} %collective-permute-done.9.partner_ref, bf16[64,32]{1,0:T(8,128)(2,1)S(1)} %collective-permute-done.10.straight_ref, ...), custom_call_target="tpu_custom_call" | custom-call | tf_op jit(solution)/shard_map/pallas_call | solution.py:389
  (23 shorter events, 3.5 us)
Async XLA Ops:
  8.4 10.2 %collective-permute-start.2 = (bf16[2,128,256]{2,1,0:T(8,128)(2,1)S(1)}, bf16[2,128,256]{2,1,0:T(8,128)(2,1)S(1)}, u32[]{:S(2)}, u32[]{:S(2)}) collective-permute-start(bf16[2,128,256]{2,1,0:T(8,128)(2,1)S(1)} %get-tuple-element.25.own_ref), channel_id=1, source_target_pairs={{0,4},{1,29},{2,6},{3,31},{4,8},{5,1},{6,10},{7,3},{8,12},{9,5},{1... | collective-permute-start | bytes 393224 | tf_op jit(solution)/shard_map/ppermute | solution.py:430
  14.8 6.9 %collective-permute-start.1 = (bf16[2,128,256]{2,1,0:T(8,128)(2,1)S(1)}, bf16[2,128,256]{2,1,0:T(8,128)(2,1)S(1)}, u32[]{:S(2)}, u32[]{:S(2)}) collective-permute-start(bf16[2,128,256]{2,1,0:T(8,128)(2,1)S(1)} %get-tuple-element.25.own_ref), channel_id=1, source_target_pairs={{0,2},{1,31},{2,4},{3,1},{4,6},{5,3},{6,8},{7,5},{8,10},{9,7},{10,... | collective-permute-start | bytes 393224 | tf_op jit(solution)/shard_map/ppermute | solution.py:430
  21.7 12.8 %collective-permute-start.4 = (bf16[4,128,256]{2,1,0:T(8,128)(2,1)S(1)}, bf16[4,128,256]{2,1,0:T(8,128)(2,1)S(1)}, u32[]{:S(2)}, u32[]{:S(2)}) collective-permute-start(bf16[4,128,256]{2,1,0:T(8,128)(2,1)S(1)} %shard_map.120.refs_0_), channel_id=1, source_target_pairs={{0,4},{1,29},{2,6},{3,31},{4,8},{5,1},{6,10},{7,3},{8,12},{9,5},{1... | collective-permute-start | bytes 786440 | tf_op jit(solution)/shard_map/ppermute | solution.py:430
  34.5 13.1 %collective-permute-start.6 = (bf16[4,128,256]{2,1,0:T(8,128)(2,1)S(1)}, bf16[4,128,256]{2,1,0:T(8,128)(2,1)S(1)}, u32[]{:S(2)}, u32[]{:S(2)}) collective-permute-start(bf16[4,128,256]{2,1,0:T(8,128)(2,1)S(1)} %collective-permute-done.4.refs_1_), channel_id=1, source_target_pairs={{0,4},{1,29},{2,6},{3,31},{4,8},{5,1},{6,10},{7,3},{8,12},{9,5},{1... | collective-permute-start | bytes 786440 | tf_op jit(solution)/shard_map/ppermute | solution.py:430
  47.6 31.1 %collective-permute-start.8 = (bf16[12,128,256]{2,1,0:T(8,128)(2,1)S(1)}, bf16[12,128,256]{2,1,0:T(8,128)(2,1)S(1)}, u32[]{:S(2)}, u32[]{:S(2)}) collective-permute-start(bf16[12,128,256]{2,1,0:T(8,128)(2,1)S(1)} %shard_map.124), channel_id=1, source_target_pairs={{0,1},{1,0},{2,3},{3,2},{4,5},{5,4},{6,7},{7,6},{8,9},{9,8},{10,11... | collective-permute-start | bytes 2359304 | tf_op jit(solution)/shard_map/ppermute | solution.py:461
  49.6 10.6 %collective-permute-start = (bf16[128,256]{1,0:T(8,128)(2,1)S(1)}, bf16[128,256]{1,0:T(8,128)(2,1)S(1)}, u32[]{:S(2)}, u32[]{:S(2)}) collective-permute-start(bf16[128,256]{1,0:T(8,128)(2,1)S(1)} %get-tuple-element.24), channel_id=1, source_target_pairs={{0,64},{64,0},{128,192},{192,128},{1,65},{65,1},{129,193},{193,129... | collective-permute-start | bytes 196616 | tf_op jit(solution)/shard_map/ppermute | solution.py:423
  53.6 23.0 %collective-permute-start.7 = (bf16[3,128,256]{2,1,0:T(8,128)(2,1)S(1)}, bf16[3,128,256]{2,1,0:T(8,128)(2,1)S(1)}, u32[]{:S(2)}, u32[]{:S(2)}) collective-permute-start(bf16[3,128,256]{2,1,0:T(8,128)(2,1)S(1)} %shard_map.122), channel_id=1, source_target_pairs={{0,4},{1,29},{2,6},{3,31},{4,8},{5,1},{6,10},{7,3},{8,12},{9,5},{1... | collective-permute-start | bytes 589832 | tf_op jit(solution)/shard_map/ppermute | solution.py:430
  60.2 7.7 %collective-permute-start.3 = (bf16[128,256]{1,0:T(8,128)(2,1)S(1)}, bf16[128,256]{1,0:T(8,128)(2,1)S(1)}, u32[]{:S(2)}, u32[]{:S(2)}) collective-permute-start(bf16[128,256]{1,0:T(8,128)(2,1)S(1)} %add.13), channel_id=1, source_target_pairs={{0,128},{64,192},{128,0},{192,64},{1,129},{65,193},{129,1},{193,65... | collective-permute-start | bytes 196616 | tf_op jit(solution)/shard_map/ppermute | solution.py:423
  67.9 7.7 %collective-permute-start.5 = (bf16[128,256]{1,0:T(8,128)(2,1)S(1)}, bf16[128,256]{1,0:T(8,128)(2,1)S(1)}, u32[]{:S(2)}, u32[]{:S(2)}) collective-permute-start(bf16[128,256]{1,0:T(8,128)(2,1)S(1)} %add.14), channel_id=1, source_target_pairs={{0,256},{256,0},{1,257},{257,1},{2,258},{258,2},{3,259},{259,3},{4... | collective-permute-start | bytes 196616 | tf_op jit(solution)/shard_map/ppermute | solution.py:423
  78.7 19.3 %copy-start = (bf16[32,512]{1,0:T(8,128)(2,1)S(1)}, bf16[32,512]{1,0:T(8,128)(2,1)}, u32[]{:S(2)}) copy-start(bf16[32,512]{1,0:T(8,128)(2,1)} %proj_w_ref.1) | copy-start | bytes 98308
  78.7 19.3 %copy-start.1 = (f32[3,512]{1,0:T(4,128)S(1)}, f32[3,512]{1,0:T(4,128)}, u32[]{:S(2)}) copy-start(f32[3,512]{1,0:T(4,128)} %time_w_ref.1) | copy-start | bytes 18436
  78.7 19.3 %copy-start.2 = (f32[512]{0:T(512)S(1)}, f32[512]{0:T(512)}, u32[]{:S(2)}) copy-start(f32[512]{0:T(512)} %param.21) | copy-start | bytes 6148
  78.7 19.3 %copy-start.3 = (f32[512]{0:T(512)S(1)}, f32[512]{0:T(512)}, u32[]{:S(2)}) copy-start(f32[512]{0:T(512)} %param.23) | copy-start | bytes 6148
  83.8 10.5 %collective-permute-start.10 = (bf16[64,32]{1,0:T(8,128)(2,1)S(1)}, bf16[64,32]{1,0:T(8,128)(2,1)S(1)}, u32[]{:S(2)}, u32[]{:S(2)}) collective-permute-start(bf16[64,32]{1,0:T(8,128)(2,1)S(1)} %get-tuple-element.41.kept_ref), channel_id=1, source_target_pairs={{64,0},{32,96},{128,64},{96,160},{192,128},{160,224},{256,192},{22... | collective-permute-start | bytes 12296 | tf_op jit(solution)/shard_map/ppermute | solution.py:477
  88.1 7.7 %collective-permute-start.11 = (bf16[64,32]{1,0:T(8,128)(2,1)S(1)}, bf16[64,32]{1,0:T(8,128)(2,1)S(1)}, u32[]{:S(2)}, u32[]{:S(2)}) collective-permute-start(bf16[64,32]{1,0:T(8,128)(2,1)S(1)} %get-tuple-element.42), channel_id=1, source_target_pairs={{64,32},{32,64},{128,96},{96,128},{192,160},{160,192},{256,224},{2... | collective-permute-start | bytes 12296 | tf_op jit(solution)/shard_map/ppermute | solution.py:478
  92.4 5.6 %collective-permute-start.9 = (bf16[64,32]{1,0:T(8,128)(2,1)S(1)}, bf16[64,32]{1,0:T(8,128)(2,1)S(1)}, u32[]{:S(2)}, u32[]{:S(2)}) collective-permute-start(bf16[64,32]{1,0:T(8,128)(2,1)S(1)} %get-tuple-element.42), channel_id=1, source_target_pairs={{0,32},{32,0},{1,33},{33,1},{2,34},{34,2},{3,35},{35,3},{4,36},{36... | collective-permute-start | bytes 12296 | tf_op jit(solution)/shard_map/ppermute | solution.py:476
where the time goes:
time: 100 us; the launch traced here: 99.5 us
  starting transfers between devices  53.1 us (53%)
  waiting for transfers between devices  26.4 us (26%)
  Pallas kernels  11.5 us (12%)
  blocking collectives  8.25 us (8%)
    ppermute x5, starting transfers between devices, along(): return lax.ppermute(block, ('z', 'c'), pairs)  29.7 us
    ppermute x5, waiting for transfers between devices, along(): return lax.ppermute(block, ('z', 'c'), pairs)  14.9 us
    ppermute x3, starting transfers between devices, flip(): lax.ppermute(v, axis, [(i, i ^ step) for i in range(count)])  11 us
    ppermute x3, waiting for transfers between devices, flip(): lax.ppermute(v, axis, [(i, i ^ step) for i in range(count)])  7.8 us
    all_gather x1, blocking collectives, one_device(): gathered = lax.all_gather(message, ('xl', 'c'), axis=0)  6.17 us
    pallas_call x1, Pallas kernels, pooled_costs(): pl.pallas_call(functools.partial(cost_kernel, MAP // 4), out_shape=(jax.S...  5.03 us
    ppermute x1, starting transfers between devices, one_device(): straight = lax.ppermute(kept, ('xh', 'y', 'xl'), frame_pairs(False))  4.33 us
    ppermute x1, starting transfers between devices, one_device(): crossed = lax.ppermute(sent, ('xh', 'y', 'xl'), frame_pairs(True))  4.24 us
  transfers between devices with their start and end apart: 12, of which 7 were waited for; matrix products, arithmetic and copies ran while one was open for 0% of the time, Pallas kernels for 3%

commit v1 on v0

--- a/solution.py
+++ b/solution.py
@@ -233,7 +233,7 @@
 
 
 def corr_kernel(z_count, where_ref, q_ref, own_ref, *refs):
-    *mine_refs, corr = refs
+    *mine_refs, cross_ref, corr = refs
     z = where_ref[1]
     toward = 2 * where_ref[3] - 1
     q = q_ref[...]
@@ -244,6 +244,9 @@
         for k in range(0, ref.shape[0], 2):
             distance += 1
             correlate(corr, q, z, z_count, ref[k], ref[k + 1], toward * distance)
+            other = 2 * distance - 2
+            low, high = cross_ref[other], cross_ref[other + 1]
+            correlate(corr, q, z, z_count, low, high, -toward * distance)
 
 
 def partial_corr(where, queries, own, blocks):
@@ -261,22 +264,19 @@
     )(where, queries, own, *blocks)
 
 
-def cost_kernel(z_count, where_ref, q_ref, last_ref, old_ref, cross_ref, *refs):
+def cost_kernel(z_count, where_ref, q_ref, last_ref, old_ref, *refs):
     del old_ref
     a_ref, b_ref, bias1_ref, bias2_ref, kept_ref, sent_ref, corr, hid, acc = refs
     z = where_ref[1]
     n = q_ref.shape[0]
     hid[0, :, 0:ROW1] = jnp.zeros((n, ROW1), BF)
     q = q_ref[...]
-    away = 1 - 2 * where_ref[3]
-    for k in range(0, cross_ref.shape[0], 2):
-        correlate(corr, q, z, z_count, cross_ref[k], cross_ref[k + 1], away * (k // 2 + 1))
     correlate(corr, q, z, z_count, last_ref[0], last_ref[1], -7)
     correlate(corr, q, z, z_count, last_ref[3], last_ref[4], 7)
     correlate(corr, q, z, z_count, last_ref[2], last_ref[5], 8)
 
     bias1 = bias1_ref[...]
-    rows1 = 8
+    rows1 = 16
     for t in range(HALF1 // rows1):
         lhs = corr[rows1 * t : rows1 * (t + 1)].reshape(rows1 * n, 256)
         got = jnp.dot(lhs, a_ref[...], preferred_element_type=F32)
@@ -292,7 +292,7 @@
 
     bias2 = bias2_ref[...]
     half = ROW2 // 2
-    rows2 = 4
+    rows2 = 8
     acc[...] = jnp.zeros(acc.shape, F32)
     for t in range(HALF2 // rows2):
         tile = slice(rows2 * t, rows2 * (t + 1))
@@ -320,14 +320,14 @@
     sent_ref[...] = pooled[n // 2 :]
 
 
-def pooled_costs(where, queries, last, corr, cross, a, b, bias1, bias2):
+def pooled_costs(where, queries, last, corr, a, b, bias1, bias2):
     n = queries.shape[0]
     vmem = pl.BlockSpec(memory_space=pltpu.VMEM)
     return pl.pallas_call(
         functools.partial(cost_kernel, MAP // 4),
         out_shape=(jax.ShapeDtypeStruct((n // 2, CH2), BF),) * 2
         + (jax.ShapeDtypeStruct(corr.shape, BF),),
-        in_specs=[pl.BlockSpec(memory_space=pltpu.SMEM)] + [vmem] * 8,
+        in_specs=[pl.BlockSpec(memory_space=pltpu.SMEM)] + [vmem] * 7,
         out_specs=(vmem,) * 3,
         scratch_shapes=[
             pltpu.VMEM((HALF2 + 1, n, 3 * ROW1), BF),
@@ -339,7 +339,7 @@
         ),
         compiler_params=pltpu.CompilerParams(vmem_limit_bytes=28 << 20),
         interpret=INTERPRET,
-    )(where, queries, last, corr, cross, a, b, bias1, bias2)[:2]
+    )(where, queries, last, corr, a, b, bias1, bias2)[:2]
 
 
 def tail_kernel(
@@ -459,10 +459,10 @@
     end = trimmed(where, ring[2])
     last = along(end, 2)
     cross = lax.ppermute(joined(*ring), "c", swap)
-    corr = partial_corr(where, queries, own, ring)
+    corr = partial_corr(where, queries, own, ring + [cross])
     last, corr = lax.optimization_barrier((last, corr))
 
-    kept, sent = pooled_costs(where, queries, both(last), corr, cross, *weights)
+    kept, sent = pooled_costs(where, queries, both(last), corr, *weights)
 
     def frame_pairs(cross):
         pairs = []

time: 100 us -> 100 us (level)
  no operation moved by 1% of the time
where the time goes in v1:
time: 100 us; the launch traced here: 99.7 us
  starting transfers between devices  53.1 us (53%)
  waiting for transfers between devices  26.4 us (26%)
  Pallas kernels  11.6 us (12%)
  blocking collectives  8.25 us (8%)
    ppermute x5, starting transfers between devices, along(): return lax.ppermute(block, ('z', 'c'), pairs)  29.7 us
    ppermute x5, waiting for transfers between devices, along(): return lax.ppermute(block, ('z', 'c'), pairs)  14.9 us
    ppermute x3, starting transfers between devices, flip(): lax.ppermute(v, axis, [(i, i ^ step) for i in range(count)])  11 us
    ppermute x3, waiting for transfers between devices, flip(): lax.ppermute(v, axis, [(i, i ^ step) for i in range(count)])  7.8 us
    all_gather x1, blocking collectives, one_device(): gathered = lax.all_gather(message, ('xl', 'c'), axis=0)  6.17 us
    pallas_call x1, Pallas kernels, pooled_costs(): pl.pallas_call(functools.partial(cost_kernel, MAP // 4), out_shape=(jax.S...  4.91 us
    ppermute x1, starting transfers between devices, one_device(): straight = lax.ppermute(kept, ('xh', 'y', 'xl'), frame_pairs(False))  4.32 us
    ppermute x1, starting transfers between devices, one_device(): crossed = lax.ppermute(sent, ('xh', 'y', 'xl'), frame_pairs(True))  4.24 us
  transfers between devices with their start and end apart: 12, of which 7 were waited for; matrix products, arithmetic and copies ran while one was open for 0% of the time, Pallas kernels for 3%

profile of v1, /device:TPU:68, one launch (start us, length us, event | category | flops | bytes accessed | tf_op | source)
XLA Modules:
  0.0 99.7 jit_solution(9174020951416667352)
XLA Ops:
  0.1 1.6 %shard_map.118 = bf16[192,256]{1,0:T(8,128)(2,1)S(1)} custom-call(s32[4]{0:T(128)S(1)} %pad_add_fusion.where_ref, bf16[2,64,256]{2,1,0:T(8,128)(2,1)} %maps_hbm.1, bf16[1,64,256]{2,1,0:T(8,128)(2,1)} %table_hbm.1, s32[1,64]{1,0:T(1,128)} %bitcast.16, s32[1,64]{1,0:T(1,128)} %bitcast.17), custom_call_target="tpu_custom_call" | custom-call | flops 2000000 | bytes 200000 | tf_op jit(solution)/shard_map/pallas_call | solution.py:64
  1.7 6.2 %all-gather = bf16[768,256]{1,0:T(8,128)(2,1)S(1)} all-gather(bf16[192,256]{1,0:T(8,128)(2,1)S(1)} %shard_map.118), channel_id=2, replica_groups=mesh['xh'=2,'y'=4,'xl'=2,'z'=16,'c'=2] {'xl','c'}, dimensions={0}, use_global_device_ids=true | all-gather | bytes 491520 | tf_op jit(solution)/shard_map/all_gather | solution.py:439
  8.4 6.4 %collective-permute-start.2 = (bf16[2,128,256]{2,1,0:T(8,128)(2,1)S(1)}, bf16[2,128,256]{2,1,0:T(8,128)(2,1)S(1)}, u32[]{:S(2)}, u32[]{:S(2)}) collective-permute-start(bf16[2,128,256]{2,1,0:T(8,128)(2,1)S(1)} %get-tuple-element.25.own_ref), channel_id=1, source_target_pairs={{0,4},{1,29},{2,6},{3,31},{4,8},{5,1},{6,10},{7,3},{8,12},{9,5},{1... | collective-permute-start | bytes 393224 | tf_op jit(solution)/shard_map/ppermute | solution.py:430
  14.8 3.8 %collective-permute-start.1 = (bf16[2,128,256]{2,1,0:T(8,128)(2,1)S(1)}, bf16[2,128,256]{2,1,0:T(8,128)(2,1)S(1)}, u32[]{:S(2)}, u32[]{:S(2)}) collective-permute-start(bf16[2,128,256]{2,1,0:T(8,128)(2,1)S(1)} %get-tuple-element.25.own_ref), channel_id=1, source_target_pairs={{0,2},{1,31},{2,4},{3,1},{4,6},{5,3},{6,8},{7,5},{8,10},{9,7},{10,... | collective-permute-start | bytes 393224 | tf_op jit(solution)/shard_map/ppermute | solution.py:430
  18.6 3.0 %collective-permute-done.1.refs_0_ = bf16[2,128,256]{2,1,0:T(8,128)(2,1)S(1)} collective-permute-done((bf16[2,128,256]{2,1,0:T(8,128)(2,1)S(1)}, bf16[2,128,256]{2,1,0:T(8,128)(2,1)S(1)}, u32[]{:S(2)}, u32[]{:S(2)}) %collective-permute-start.1) | collective-permute-done | bytes 131104 | tf_op jit(solution)/shard_map/ppermute | solution.py:430
  21.7 6.4 %collective-permute-start.4 = (bf16[4,128,256]{2,1,0:T(8,128)(2,1)S(1)}, bf16[4,128,256]{2,1,0:T(8,128)(2,1)S(1)}, u32[]{:S(2)}, u32[]{:S(2)}) collective-permute-start(bf16[4,128,256]{2,1,0:T(8,128)(2,1)S(1)} %shard_map.120.refs_0_), channel_id=1, source_target_pairs={{0,4},{1,29},{2,6},{3,31},{4,8},{5,1},{6,10},{7,3},{8,12},{9,5},{1... | collective-permute-start | bytes 786440 | tf_op jit(solution)/shard_map/ppermute | solution.py:430
  29.2 5.3 %collective-permute-done.4.refs_1_ = bf16[4,128,256]{2,1,0:T(8,128)(2,1)S(1)} collective-permute-done((bf16[4,128,256]{2,1,0:T(8,128)(2,1)S(1)}, bf16[4,128,256]{2,1,0:T(8,128)(2,1)S(1)}, u32[]{:S(2)}, u32[]{:S(2)}) %collective-permute-start.4) | collective-permute-done | bytes 262176 | tf_op jit(solution)/shard_map/ppermute | solution.py:430
  34.5 6.5 %collective-permute-start.6 = (bf16[4,128,256]{2,1,0:T(8,128)(2,1)S(1)}, bf16[4,128,256]{2,1,0:T(8,128)(2,1)S(1)}, u32[]{:S(2)}, u32[]{:S(2)}) collective-permute-start(bf16[4,128,256]{2,1,0:T(8,128)(2,1)S(1)} %collective-permute-done.4.refs_1_), channel_id=1, source_target_pairs={{0,4},{1,29},{2,6},{3,31},{4,8},{5,1},{6,10},{7,3},{8,12},{9,5},{1... | collective-permute-start | bytes 786440 | tf_op jit(solution)/shard_map/ppermute | solution.py:430
  41.0 6.6 %collective-permute-done.6.blocks_ref.refs_2_ = bf16[4,128,256]{2,1,0:T(8,128)(2,1)S(1)} collective-permute-done((bf16[4,128,256]{2,1,0:T(8,128)(2,1)S(1)}, bf16[4,128,256]{2,1,0:T(8,128)(2,1)S(1)}, u32[]{:S(2)}, u32[]{:S(2)}) %collective-permute-start.6) | collective-permute-done | bytes 262176 | tf_op jit(solution)/shard_map/ppermute | solution.py:430
  47.6 1.9 %collective-permute-start.8 = (bf16[12,128,256]{2,1,0:T(8,128)(2,1)S(1)}, bf16[12,128,256]{2,1,0:T(8,128)(2,1)S(1)}, u32[]{:S(2)}, u32[]{:S(2)}) collective-permute-start(bf16[12,128,256]{2,1,0:T(8,128)(2,1)S(1)} %shard_map.123), channel_id=1, source_target_pairs={{0,1},{1,0},{2,3},{3,2},{4,5},{5,4},{6,7},{7,6},{8,9},{9,8},{10,11... | collective-permute-start | bytes 2359304 | tf_op jit(solution)/shard_map/ppermute | solution.py:461
  49.6 3.5 %collective-permute-start = (bf16[128,256]{1,0:T(8,128)(2,1)S(1)}, bf16[128,256]{1,0:T(8,128)(2,1)S(1)}, u32[]{:S(2)}, u32[]{:S(2)}) collective-permute-start(bf16[128,256]{1,0:T(8,128)(2,1)S(1)} %get-tuple-element.24), channel_id=1, source_target_pairs={{0,64},{64,0},{128,192},{192,128},{1,65},{65,1},{129,193},{193,129... | collective-permute-start | bytes 196616 | tf_op jit(solution)/shard_map/ppermute | solution.py:423
  53.6 6.6 %collective-permute-start.7 = (bf16[3,128,256]{2,1,0:T(8,128)(2,1)S(1)}, bf16[3,128,256]{2,1,0:T(8,128)(2,1)S(1)}, u32[]{:S(2)}, u32[]{:S(2)}) collective-permute-start(bf16[3,128,256]{2,1,0:T(8,128)(2,1)S(1)} %shard_map.122), channel_id=1, source_target_pairs={{0,4},{1,29},{2,6},{3,31},{4,8},{5,1},{6,10},{7,3},{8,12},{9,5},{1... | collective-permute-start | bytes 589832 | tf_op jit(solution)/shard_map/ppermute | solution.py:430
  60.2 4.8 %collective-permute-start.3 = (bf16[128,256]{1,0:T(8,128)(2,1)S(1)}, bf16[128,256]{1,0:T(8,128)(2,1)S(1)}, u32[]{:S(2)}, u32[]{:S(2)}) collective-permute-start(bf16[128,256]{1,0:T(8,128)(2,1)S(1)} %add.13), channel_id=1, source_target_pairs={{0,128},{64,192},{128,0},{192,64},{1,129},{65,193},{129,1},{193,65... | collective-permute-start | bytes 196616 | tf_op jit(solution)/shard_map/ppermute | solution.py:423
  65.0 2.8 %collective-permute-done.3 = bf16[128,256]{1,0:T(8,128)(2,1)S(1)} collective-permute-done((bf16[128,256]{1,0:T(8,128)(2,1)S(1)}, bf16[128,256]{1,0:T(8,128)(2,1)S(1)}, u32[]{:S(2)}, u32[]{:S(2)}) %collective-permute-start.3) | collective-permute-done | bytes 65568 | tf_op jit(solution)/shard_map/ppermute | solution.py:423
  67.9 2.7 %collective-permute-start.5 = (bf16[128,256]{1,0:T(8,128)(2,1)S(1)}, bf16[128,256]{1,0:T(8,128)(2,1)S(1)}, u32[]{:S(2)}, u32[]{:S(2)}) collective-permute-start(bf16[128,256]{1,0:T(8,128)(2,1)S(1)} %add.14), channel_id=1, source_target_pairs={{0,256},{256,0},{1,257},{257,1},{2,258},{258,2},{3,259},{259,3},{4... | collective-permute-start | bytes 196616 | tf_op jit(solution)/shard_map/ppermute | solution.py:423
  70.6 4.9 %collective-permute-done.5 = bf16[128,256]{1,0:T(8,128)(2,1)S(1)} collective-permute-done((bf16[128,256]{1,0:T(8,128)(2,1)S(1)}, bf16[128,256]{1,0:T(8,128)(2,1)S(1)}, u32[]{:S(2)}, u32[]{:S(2)}) %collective-permute-start.5) | collective-permute-done | bytes 65568 | tf_op jit(solution)/shard_map/ppermute | solution.py:423
  76.9 2.1 %all_gather.11.last_ref = bf16[6,128,256]{2,1,0:T(8,128)(2,1)S(1)} all-gather(bf16[3,128,256]{2,1,0:T(8,128)(2,1)S(1)} %collective-permute-done.7), channel_id=1, replica_groups=mesh['xh'=2,'y'=4,'xl'=2,'z'=16,'c'=2] {'c'}, dimensions={0}, use_global_device_ids=true | all-gather | bytes 589824 | tf_op jit(solution)/shard_map/all_gather | solution.py:433
  79.0 4.9 %shard_map.125 = (bf16[64,32]{1,0:T(8,128)(2,1)S(1)}, bf16[64,32]{1,0:T(8,128)(2,1)S(1)}, bf16[33,128,256]{2,1,0:T(8,128)(2,1)S(1)}) custom-call(s32[4]{0:T(128)S(1)} %pad_add_fusion.where_ref, bf16[128,256]{1,0:T(8,128)(2,1)S(1)} %add.15.q_ref, bf16[6,128,256]{2,1,0:T(8,128)(2,1)S(1)} %all_gather.11.last_ref, ...), custom_call_target="tpu_custom_call", output_to_operand_aliasing={{2}: (3, {})} | custom-call | flops 5000000000 | bytes 4000000 | tf_op jit(solution)/shard_map/pallas_call | solution.py:326
  83.9 4.3 %collective-permute-start.10 = (bf16[64,32]{1,0:T(8,128)(2,1)S(1)}, bf16[64,32]{1,0:T(8,128)(2,1)S(1)}, u32[]{:S(2)}, u32[]{:S(2)}) collective-permute-start(bf16[64,32]{1,0:T(8,128)(2,1)S(1)} %get-tuple-element.41.kept_ref), channel_id=1, source_target_pairs={{64,0},{32,96},{128,64},{96,160},{192,128},{160,224},{256,192},{22... | collective-permute-start | bytes 12296 | tf_op jit(solution)/shard_map/ppermute | solution.py:477
  88.3 4.2 %collective-permute-start.11 = (bf16[64,32]{1,0:T(8,128)(2,1)S(1)}, bf16[64,32]{1,0:T(8,128)(2,1)S(1)}, u32[]{:S(2)}, u32[]{:S(2)}) collective-permute-start(bf16[64,32]{1,0:T(8,128)(2,1)S(1)} %get-tuple-element.42), channel_id=1, source_target_pairs={{64,32},{32,64},{128,96},{96,128},{192,160},{160,192},{256,224},{2... | collective-permute-start | bytes 12296 | tf_op jit(solution)/shard_map/ppermute | solution.py:478
  92.5 1.9 %collective-permute-start.9 = (bf16[64,32]{1,0:T(8,128)(2,1)S(1)}, bf16[64,32]{1,0:T(8,128)(2,1)S(1)}, u32[]{:S(2)}, u32[]{:S(2)}) collective-permute-start(bf16[64,32]{1,0:T(8,128)(2,1)S(1)} %get-tuple-element.42), channel_id=1, source_target_pairs={{0,32},{32,0},{1,33},{33,1},{2,34},{34,2},{3,35},{35,3},{4,36},{36... | collective-permute-start | bytes 12296 | tf_op jit(solution)/shard_map/ppermute | solution.py:476
  94.4 1.6 %collective-permute-done.11.crossed_ref = bf16[64,32]{1,0:T(8,128)(2,1)S(1)} collective-permute-done((bf16[64,32]{1,0:T(8,128)(2,1)S(1)}, bf16[64,32]{1,0:T(8,128)(2,1)S(1)}, u32[]{:S(2)}, u32[]{:S(2)}) %collective-permute-start.11) | collective-permute-done | bytes 4128 | tf_op jit(solution)/shard_map/ppermute | solution.py:478
  96.0 2.1 %collective-permute-done.9.partner_ref = bf16[64,32]{1,0:T(8,128)(2,1)S(1)} collective-permute-done((bf16[64,32]{1,0:T(8,128)(2,1)S(1)}, bf16[64,32]{1,0:T(8,128)(2,1)S(1)}, u32[]{:S(2)}, u32[]{:S(2)}) %collective-permute-start.9) | collective-permute-done | bytes 4128 | tf_op jit(solution)/shard_map/ppermute | solution.py:476
  98.2 1.5 %shard_map.126 = bf16[64,2,512]{2,1,0:T(2,128)(2,1)} custom-call(s32[4]{0:T(128)S(1)} %pad_add_fusion.where_ref, bf16[64,32]{1,0:T(8,128)(2,1)S(1)} %get-tuple-element.41.kept_ref, bf16[64,32]{1,0:T(8,128)(2,1)S(1)} %collective-permute-done.9.partner_ref, bf16[64,32]{1,0:T(8,128)(2,1)S(1)} %collective-permute-done.10.straight_ref, ...), custom_call_target="tpu_custom_call" | custom-call | tf_op jit(solution)/shard_map/pallas_call | solution.py:389
  (23 shorter events, 3.8 us)
Async XLA Ops:
  8.4 10.2 %collective-permute-start.2 = (bf16[2,128,256]{2,1,0:T(8,128)(2,1)S(1)}, bf16[2,128,256]{2,1,0:T(8,128)(2,1)S(1)}, u32[]{:S(2)}, u32[]{:S(2)}) collective-permute-start(bf16[2,128,256]{2,1,0:T(8,128)(2,1)S(1)} %get-tuple-element.25.own_ref), channel_id=1, source_target_pairs={{0,4},{1,29},{2,6},{3,31},{4,8},{5,1},{6,10},{7,3},{8,12},{9,5},{1... | collective-permute-start | bytes 393224 | tf_op jit(solution)/shard_map/ppermute | solution.py:430
  14.8 6.9 %collective-permute-start.1 = (bf16[2,128,256]{2,1,0:T(8,128)(2,1)S(1)}, bf16[2,128,256]{2,1,0:T(8,128)(2,1)S(1)}, u32[]{:S(2)}, u32[]{:S(2)}) collective-permute-start(bf16[2,128,256]{2,1,0:T(8,128)(2,1)S(1)} %get-tuple-element.25.own_ref), channel_id=1, source_target_pairs={{0,2},{1,31},{2,4},{3,1},{4,6},{5,3},{6,8},{7,5},{8,10},{9,7},{10,... | collective-permute-start | bytes 393224 | tf_op jit(solution)/shard_map/ppermute | solution.py:430
  21.7 12.8 %collective-permute-start.4 = (bf16[4,128,256]{2,1,0:T(8,128)(2,1)S(1)}, bf16[4,128,256]{2,1,0:T(8,128)(2,1)S(1)}, u32[]{:S(2)}, u32[]{:S(2)}) collective-permute-start(bf16[4,128,256]{2,1,0:T(8,128)(2,1)S(1)} %shard_map.120.refs_0_), channel_id=1, source_target_pairs={{0,4},{1,29},{2,6},{3,31},{4,8},{5,1},{6,10},{7,3},{8,12},{9,5},{1... | collective-permute-start | bytes 786440 | tf_op jit(solution)/shard_map/ppermute | solution.py:430
  34.5 13.1 %collective-permute-start.6 = (bf16[4,128,256]{2,1,0:T(8,128)(2,1)S(1)}, bf16[4,128,256]{2,1,0:T(8,128)(2,1)S(1)}, u32[]{:S(2)}, u32[]{:S(2)}) collective-permute-start(bf16[4,128,256]{2,1,0:T(8,128)(2,1)S(1)} %collective-permute-done.4.refs_1_), channel_id=1, source_target_pairs={{0,4},{1,29},{2,6},{3,31},{4,8},{5,1},{6,10},{7,3},{8,12},{9,5},{1... | collective-permute-start | bytes 786440 | tf_op jit(solution)/shard_map/ppermute | solution.py:430
  47.6 28.0 %collective-permute-start.8 = (bf16[12,128,256]{2,1,0:T(8,128)(2,1)S(1)}, bf16[12,128,256]{2,1,0:T(8,128)(2,1)S(1)}, u32[]{:S(2)}, u32[]{:S(2)}) collective-permute-start(bf16[12,128,256]{2,1,0:T(8,128)(2,1)S(1)} %shard_map.123), channel_id=1, source_target_pairs={{0,1},{1,0},{2,3},{3,2},{4,5},{5,4},{6,7},{7,6},{8,9},{9,8},{10,11... | collective-permute-start | bytes 2359304 | tf_op jit(solution)/shard_map/ppermute | solution.py:461
  49.6 10.6 %collective-permute-start = (bf16[128,256]{1,0:T(8,128)(2,1)S(1)}, bf16[128,256]{1,0:T(8,128)(2,1)S(1)}, u32[]{:S(2)}, u32[]{:S(2)}) collective-permute-start(bf16[128,256]{1,0:T(8,128)(2,1)S(1)} %get-tuple-element.24), channel_id=1, source_target_pairs={{0,64},{64,0},{128,192},{192,128},{1,65},{65,1},{129,193},{193,129... | collective-permute-start | bytes 196616 | tf_op jit(solution)/shard_map/ppermute | solution.py:423
  53.6 23.3 %collective-permute-start.7 = (bf16[3,128,256]{2,1,0:T(8,128)(2,1)S(1)}, bf16[3,128,256]{2,1,0:T(8,128)(2,1)S(1)}, u32[]{:S(2)}, u32[]{:S(2)}) collective-permute-start(bf16[3,128,256]{2,1,0:T(8,128)(2,1)S(1)} %shard_map.122), channel_id=1, source_target_pairs={{0,4},{1,29},{2,6},{3,31},{4,8},{5,1},{6,10},{7,3},{8,12},{9,5},{1... | collective-permute-start | bytes 589832 | tf_op jit(solution)/shard_map/ppermute | solution.py:430
  60.2 7.7 %collective-permute-start.3 = (bf16[128,256]{1,0:T(8,128)(2,1)S(1)}, bf16[128,256]{1,0:T(8,128)(2,1)S(1)}, u32[]{:S(2)}, u32[]{:S(2)}) collective-permute-start(bf16[128,256]{1,0:T(8,128)(2,1)S(1)} %add.13), channel_id=1, source_target_pairs={{0,128},{64,192},{128,0},{192,64},{1,129},{65,193},{129,1},{193,65... | collective-permute-start | bytes 196616 | tf_op jit(solution)/shard_map/ppermute | solution.py:423
  67.9 7.7 %collective-permute-start.5 = (bf16[128,256]{1,0:T(8,128)(2,1)S(1)}, bf16[128,256]{1,0:T(8,128)(2,1)S(1)}, u32[]{:S(2)}, u32[]{:S(2)}) collective-permute-start(bf16[128,256]{1,0:T(8,128)(2,1)S(1)} %add.14), channel_id=1, source_target_pairs={{0,256},{256,0},{1,257},{257,1},{2,258},{258,2},{3,259},{259,3},{4... | collective-permute-start | bytes 196616 | tf_op jit(solution)/shard_map/ppermute | solution.py:423
  79.0 19.1 %copy-start = (bf16[32,512]{1,0:T(8,128)(2,1)S(1)}, bf16[32,512]{1,0:T(8,128)(2,1)}, u32[]{:S(2)}) copy-start(bf16[32,512]{1,0:T(8,128)(2,1)} %proj_w_ref.1) | copy-start | bytes 98308
  79.0 19.1 %copy-start.1 = (f32[3,512]{1,0:T(4,128)S(1)}, f32[3,512]{1,0:T(4,128)}, u32[]{:S(2)}) copy-start(f32[3,512]{1,0:T(4,128)} %time_w_ref.1) | copy-start | bytes 18436
  79.0 19.1 %copy-start.2 = (f32[512]{0:T(512)S(1)}, f32[512]{0:T(512)}, u32[]{:S(2)}) copy-start(f32[512]{0:T(512)} %param.21) | copy-start | bytes 6148
  79.0 19.1 %copy-start.3 = (f32[512]{0:T(512)S(1)}, f32[512]{0:T(512)}, u32[]{:S(2)}) copy-start(f32[512]{0:T(512)} %param.23) | copy-start | bytes 6148
  83.9 10.5 %collective-permute-start.10 = (bf16[64,32]{1,0:T(8,128)(2,1)S(1)}, bf16[64,32]{1,0:T(8,128)(2,1)S(1)}, u32[]{:S(2)}, u32[]{:S(2)}) collective-permute-start(bf16[64,32]{1,0:T(8,128)(2,1)S(1)} %get-tuple-element.41.kept_ref), channel_id=1, source_target_pairs={{64,0},{32,96},{128,64},{96,160},{192,128},{160,224},{256,192},{22... | collective-permute-start | bytes 12296 | tf_op jit(solution)/shard_map/ppermute | solution.py:477
  88.3 7.7 %collective-permute-start.11 = (bf16[64,32]{1,0:T(8,128)(2,1)S(1)}, bf16[64,32]{1,0:T(8,128)(2,1)S(1)}, u32[]{:S(2)}, u32[]{:S(2)}) collective-permute-start(bf16[64,32]{1,0:T(8,128)(2,1)S(1)} %get-tuple-element.42), channel_id=1, source_target_pairs={{64,32},{32,64},{128,96},{96,128},{192,160},{160,192},{256,224},{2... | collective-permute-start | bytes 12296 | tf_op jit(solution)/shard_map/ppermute | solution.py:478
  92.5 5.6 %collective-permute-start.9 = (bf16[64,32]{1,0:T(8,128)(2,1)S(1)}, bf16[64,32]{1,0:T(8,128)(2,1)S(1)}, u32[]{:S(2)}, u32[]{:S(2)}) collective-permute-start(bf16[64,32]{1,0:T(8,128)(2,1)S(1)} %get-tuple-element.42), channel_id=1, source_target_pairs={{0,32},{32,0},{1,33},{33,1},{2,34},{34,2},{3,35},{35,3},{4,36},{36... | collective-permute-start | bytes 12296 | tf_op jit(solution)/shard_map/ppermute | solution.py:476
